TPU v7x, 32 devices: a whole 2x2x4 slice. The times are simulated.
32 devices in a mesh: trial: 8 (over z, y), tensor: 4 (over x, core).
Axes of the slice: x: 2, y: 2, z: 4, core: 2. Of those that a mesh axis runs over, the one named last changes fastest.
Arguments:
- stored_attention: bfloat16 [8, 1024, 8192], P('trial', None, 'tensor'), may hold values from -6 to 6
- output_gradient: bfloat16 [8, 1024, 8192], P('trial', 'tensor'), may hold values from -6 to 6
- output_weight: bfloat16 [8192, 8192], P('tensor', 'trial'), may hold values from -0.0625 to 0.0625
- down_adapter: bfloat16 [8, 8192, 128], P('trial', 'tensor'), may hold values from -0.0625 to 0.0625
- up_adapter: bfloat16 [8, 128, 8192], P('trial'), may hold values from -0.0625 to 0.0625
- lengths: int32 [8], P('trial'), may hold values from 128 to 1024, as said below
- ranks: int32 [8], P('trial'), may hold values from 16 to 128, as said below
Outputs:
- attention_gradient: bfloat16 [8, 1024, 8192], P('trial', None, 'tensor')
- down_gradient: float32 [8, 8192, 128], P('trial', 'tensor')
- up_gradient: float32 [8, 128, 8192], P('trial', None, 'tensor')
Inputs may be any that keep to these rules, and one draw needn't show every extreme that they name: `lengths`: rows at or beyond a trial's count are padding; some trial has all 1024 rows live. `ranks`: each rank is a multiple of 16; some trial has rank 128 and some has 16.
All inputs are finite; a program needn't handle non-finite values.
Results may differ from a plain program's by a relative error of at most 0.0034.
Values may be sent and summed in bfloat16 or wider, within the bound.
A program may use at most 128 MiB of HBM per device.

v0:
```python
import jax
import jax.numpy as jnp
from jax import lax
from jax.sharding import PartitionSpec as P

adapter_alpha = 32.0


def row_product(left, right):
    return jnp.einsum("tk,hk->th", left, right, preferred_element_type=jnp.float32)


def body(
    stored_attention, output_gradient, output_weight, down_adapter, up_adapter, lengths, ranks
):
    attention_rows = stored_attention[0]
    gradient_rows = output_gradient[0]
    down_piece = down_adapter[0]
    up_complete = up_adapter[0]
    length = lengths[0]
    adapter_rank = ranks[0]
    token_rows = attention_rows.shape[0]
    head_cols = attention_rows.shape[1]
    shard_rows = gradient_rows.shape[0]
    rank_mask = jnp.arange(up_complete.shape[0]) < adapter_rank
    adapter_scale = adapter_alpha / jnp.sqrt(adapter_rank.astype(jnp.float32))
    a_low = jnp.where(rank_mask[None, :], down_piece, jnp.zeros_like(down_piece))
    b_low = jnp.where(rank_mask[:, None], up_complete, jnp.zeros_like(up_complete))
    row_offset = lax.axis_index("tensor") * shard_rows
    live_rows = row_offset + jnp.arange(shard_rows) < length
    gradient_rows = jnp.where(live_rows[:, None], gradient_rows, jnp.zeros_like(gradient_rows))
    u_part = jnp.einsum(
        "td,rd->tr", gradient_rows, b_low, preferred_element_type=jnp.float32
    ).astype(jnp.bfloat16)
    v_partial = jnp.dot(attention_rows, a_low, preferred_element_type=jnp.float32)
    lowrank_right = lax.psum(v_partial, "tensor").astype(jnp.bfloat16)
    col_start = lax.axis_index("tensor") * head_cols
    rows_all, u_all = (
        lax.all_gather(gradient_rows, "tensor", axis=0, tiled=True),
        lax.all_gather(u_part, "tensor", axis=0, tiled=True),
    )
    dense_piece = row_product(rows_all, lax.all_gather(output_weight, "trial", axis=1, tiled=True))
    lowrank_piece = jnp.einsum("tr,hr->th", u_all, a_low, preferred_element_type=jnp.float32)
    attention_gradient = (dense_piece + adapter_scale * lowrank_piece).astype(jnp.bfloat16)
    down_total = jnp.einsum("th,tr->hr", attention_rows, u_all, preferred_element_type=jnp.float32)
    own_cols = lax.dynamic_slice_in_dim(rows_all, col_start, head_cols, 1)
    up_total = jnp.einsum("tr,th->rh", lowrank_right, own_cols, preferred_element_type=jnp.float32)
    down_gradient = adapter_scale * down_total / float(token_rows)
    up_gradient = adapter_scale * up_total / float(token_rows)
    return (attention_gradient[None], down_gradient[None], up_gradient[None])


def solution(mesh):
    placed = (
        P("trial", None, "tensor"),
        P("trial", "tensor", None),
        P("tensor", "trial"),
        P("trial", "tensor", None),
        P("trial", None, None),
        P("trial"),
        P("trial"),
    )
    return jax.shard_map(
        body,
        mesh=mesh,
        in_specs=placed,
        out_specs=(
            P("trial", None, "tensor"),
            P("trial", "tensor", None),
            P("trial", None, "tensor"),
        ),
        check_vma=False,
    )
```

profile of v0, /device:TPU:0, one launch (start us, length us, event | category | flops | bytes accessed | tf_op | source)
XLA Modules:
  0.0 825.9 jit_solution(16108703871894892472)
XLA Ops:
  7.2 0.0 all-gather.3.cloned.1.call-start
  7.9 4.5 bitcast_select_fusion
  12.4 0.0 all-gather.3.cloned.1.call-update
  12.4 0.0 all-gather.5.cloned.1.call-start
  12.5 0.7 all-gather.5.cloned.1.call-update
  13.9 0.0 copy-start
  13.9 4.3 fusion.36
  18.2 0.0 copy-start.1
  18.3 7.3 all_gather.11
  25.6 0.0 copy-done
  25.6 0.7 fusion.20
  26.3 1.3 copy.10
  27.6 0.0 copy-done.1
  27.6 4.3 fusion.33
  32.0 26.7 %all-reduce.1 = bf16[1024,128]{0,1:T(8,128)(2,1)S(1)} all-reduce(f32[1024,128]{0,1:T(8,128)S(1)} %fusion.33), channel_id=1, replica_groups=mesh['trial'=8,'tensor'=4] {'tensor'}, use_global_device_ids=true, to_apply=%region_0.1 | all-reduce | flops 131072 | bytes 786432 | tf_op jit(solution)/shard_map/psum | solution.py:36
  58.7 71.0 %all-gather.3.cloned.1.call-done = bf16[1024,8192]{1,0:T(8,128)(2,1)} async-done(((bf16[256,8192]{1,0:T(8,128)(2,1)}), bf16[1024,8192]{1,0:T(8,128)(2,1)}) %all-gather.3.cloned.1.call-update) | async-done | bytes 16777232 | tf_op jit(solution)/shard_map/all_gather | solution.py:39
  129.6 3.9 fusion.26
  133.5 635.4 %all-gather.5.cloned.1.call-done = bf16[2048,8192]{1,0:T(8,128)(2,1)} async-done(((bf16[2048,1024]{1,0:T(8,128)(2,1)}), bf16[2048,8192]{1,0:T(8,128)(2,1)}) %all-gather.5.cloned.1.call-update) | async-done | bytes 33554448 | tf_op jit(solution)/shard_map/all_gather | solution.py:42
  769.0 43.4 %fusion.53 = f32[1024,2048]{1,0:T(8,128)} fusion(bf16[1024,8192]{1,0:T(8,128)(2,1)} %all-gather.3.cloned.1.call-done, bf16[2048,8192]{1,0:T(8,128)(2,1)} %all-gather.5.cloned.1.call-done), kind=kOutput, calls=%fused_computation.40 | convolution fusion | flops 34359738368 | bytes 58720256 | tf_op jit(solution)/shard_map/tk,hk->th/dot_general | solution.py:10
  812.4 6.6 fusion.10
  (2 shorter events, 0.0 us)
Async XLA Ops:
  7.2 122.5 %all-gather.3.cloned.1.call-start = ((), (), s32[]{:S(2)}) async-start(), calls=%async_computation | async-start | bytes 20971520 | tf_op jit(solution)/shard_map/all_gather | solution.py:39
  12.4 756.5 %all-gather.5.cloned.1.call-start = ((), (), s32[]{:S(2)}) async-start(), calls=%async_computation.1 | async-start | bytes 37748736 | tf_op jit(solution)/shard_map/all_gather | solution.py:42
  13.9 11.7 %copy-start = (bf16[1,1024,2048]{2,1,0:T(8,128)(2,1)S(1)}, bf16[1,1024,2048]{2,1,0:T(8,128)(2,1)}, u32[]{:S(2)}) copy-start(bf16[1,1024,2048]{2,1,0:T(8,128)(2,1)} %param.7) | copy-start | bytes 12582916
  18.2 9.4 %copy-start.1 = (bf16[1,2048,128]{2,1,0:T(8,128)(2,1)S(1)}, bf16[1,2048,128]{2,1,0:T(8,128)(2,1)}, u32[]{:S(2)}) copy-start(bf16[1,2048,128]{2,1,0:T(8,128)(2,1)} %param.10) | copy-start | bytes 1572868
Sparse Core Ops, SparseCore 0:
  12.6 117.0 all-gather.2
  131.2 637.7 all-gather.4
where the time goes:
time: 826 us
  waiting for transfers between devices  707 us (86%)
  matrix products  63.4 us (8%)
  blocking collectives  34 us (4%)
  between operations  15.4 us (2%)
    all_gather x1, waiting for transfers between devices, body(): lax.all_gather(output_weight, 'trial', axis=1, tiled=True)  635 us
    all_gather x1, waiting for transfers between devices, body(): lax.all_gather(gradient_rows, 'tensor', axis=0, tiled=True)  71 us
    dot_general x1, matrix products, row_product(): jnp.einsum('tk,hk->th', left, right, preferred_element_type=jnp.float32)  43.4 us
    psum x1, blocking collectives, body(): lowrank_right = lax.psum(v_partial, 'tensor').astype(jnp.bfloat16)  26.7 us
  transfers between devices with their start and end apart: 2, of which 2 were waited for; matrix products, arithmetic and copies ran while one was open for 2% of the time, Pallas kernels for 0%

commit v1 on v0

--- a/solution.py
+++ b/solution.py
@@ -1,13 +1,364 @@
+import functools
+
 import jax
 import jax.numpy as jnp
 from jax import lax
+from jax.experimental import pallas as pl
+from jax.experimental.pallas import tpu as pltpu
 from jax.sharding import PartitionSpec as P
 
 adapter_alpha = 32.0
+MESH = pl.DeviceIdType.MESH
+NT = (((1,), (1,)), ((), ()))
 
 
 def row_product(left, right):
     return jnp.einsum("tk,hk->th", left, right, preferred_element_type=jnp.float32)
+
+
+def dense_kernel(
+    planes, chunks, wide,
+    dy_ref, w_ref, dense_ref, dyup_ref,
+    wv, dyv, part, prec, acc,
+    w_loc, w_up, w_dn, w_recv,
+    dy_loc, dyy_send, dyx_send, dyc_send, dy_recv,
+    p_send, p_recv, o_sem, up_sem,
+):
+    trial, s = lax.axis_index("trial"), lax.axis_index("tensor")
+    z, y = trial // 2, trial % 2
+    x, c = s // 2, s % 2
+    oy = 1 - y
+    s_c, s_x, s_xc = 2 * x + 1 - c, 2 * (1 - x) + c, 2 * (1 - x) + 1 - c
+    rows, width = dy_ref.shape[0], w_ref.shape[1]
+    tokens = dyv.shape[2]
+    head = chunks // 2
+    to_core, to_x, to_y = (trial, s_c), (trial, s_x), (2 * z + oy, s)
+    above, below = z < planes - 1, z > 0
+    inner = jnp.logical_and(above, below)
+
+    def copy(src, dst, ss, rs, dev):
+        return pltpu.make_async_remote_copy(
+            src_ref=src, dst_ref=dst, send_sem=ss, recv_sem=rs,
+            device_id=dev, device_id_type=MESH)
+
+    def w_slot(zz, n):
+        return wv.at[zz, pl.ds(pl.multiple_of(n * wide, wide), wide), :]
+
+    def w_own(n):
+        return w_ref.at[pl.ds(pl.multiple_of(n * wide, wide), wide), :]
+
+    def w_send(zz, n, up, own):
+        src = w_own(n) if own else w_slot(zz, n)
+        sem = w_up if up else w_dn
+        dev = (trial + 2, s) if up else (trial - 2, s)
+        return copy(src, w_slot(zz, n), sem.at[zz, n], w_recv.at[zz, n], dev)
+
+    def w_arrived(zz, n):
+        copy(w_slot(zz, n), w_slot(zz, n), w_up.at[zz, n], w_recv.at[zz, n], to_y).wait_recv()
+
+    def start_own(n):
+        @pl.when(above)
+        def _():
+            w_send(z, n, True, True).start()
+
+        @pl.when(below)
+        def _():
+            w_send(z, n, False, True).start()
+
+    def forward(hop, n):
+        @pl.when(jnp.logical_and(inner, z + hop < planes))
+        def _():
+            w_arrived(z + hop, n)
+            w_send(z + hop, n, False, False).start()
+
+        @pl.when(jnp.logical_and(inner, z - hop >= 0))
+        def _():
+            w_arrived(z - hop, n)
+            w_send(z - hop, n, True, False).start()
+
+    def dy_own(j, parity):
+        start = pl.multiple_of((2 * j + parity) * width, width)
+        return dy_ref.at[:, pl.ds(start, width)]
+
+    def dy_slot(yy, ss, j):
+        return dyv.at[yy, j, pl.ds(pl.multiple_of(ss * rows, rows), rows), :]
+
+    def dy_send(src, yy, ss, j, sem, dev):
+        return copy(src, dy_slot(yy, ss, j), sem, dy_recv.at[yy, ss, j], dev)
+
+    def dy_arrived(yy, ss, j):
+        slot = dy_slot(yy, ss, j)
+        dy_send(slot, yy, ss, j, dyy_send.at[j], to_y).wait_recv()
+
+    def first_copies(j):
+        return (
+            dy_send(dy_own(j, oy), y, s, j, dyy_send.at[j], to_y),
+            dy_send(dy_own(j, y), y, s, j, dyx_send.at[0, j], to_x),
+            dy_send(dy_own(j, y), y, s, j, dyc_send.at[0, j], to_core),
+        )
+
+    def local_dy(j):
+        return pltpu.make_async_copy(dy_own(j, y), dy_slot(y, s, j), dy_loc.at[j])
+
+    def local_w(n):
+        return pltpu.make_async_copy(w_own(n), w_slot(z, n), w_loc.at[n])
+
+    def later_copies(j):
+        return (
+            dy_send(dy_slot(oy, s, j), oy, s, j, dyx_send.at[1, j], to_x),
+            dy_send(dy_slot(oy, s, j), oy, s, j, dyc_send.at[1, j], to_core),
+            dy_send(dy_slot(y, s_x, j), y, s_x, j, dyc_send.at[2, j], to_core),
+            dy_send(dy_slot(oy, s_x, j), oy, s_x, j, dyc_send.at[3, j], to_core),
+        )
+
+    def partial_copy(n):
+        return copy(part.at[n], prec.at[n], p_send.at[n], p_recv.at[n], to_y)
+
+    def out_copy(n):
+        cols = pl.ds(pl.multiple_of(n * wide, wide), wide)
+        return pltpu.make_async_copy(acc.at[n % 2], dense_ref.at[:, cols], o_sem.at[n % 2])
+
+    def loop(lo, hi, fn):
+        def step(i, carry):
+            fn(i)
+            return carry
+        lax.fori_loop(lo, hi, step, 0)
+
+    barrier = pltpu.get_barrier_semaphore()
+    for dev in (to_core, to_x, to_y):
+        pl.semaphore_signal(barrier, inc=1, device_id=dev, device_id_type=MESH)
+
+    @pl.when(above)
+    def _():
+        pl.semaphore_signal(barrier, inc=1, device_id=(trial + 2, s), device_id_type=MESH)
+
+    @pl.when(below)
+    def _():
+        pl.semaphore_signal(barrier, inc=1, device_id=(trial - 2, s), device_id_type=MESH)
+
+    @pl.when(inner)
+    def _():
+        pl.semaphore_wait(barrier, 5)
+
+    @pl.when(jnp.logical_not(inner))
+    def _():
+        pl.semaphore_wait(barrier, 4)
+
+    loop(0, head, start_own)
+
+    def begin(j):
+        for item in first_copies(j):
+            item.start()
+        local_dy(j).start()
+    loop(0, planes, begin)
+    loop(0, chunks, lambda n: local_w(n).start())
+
+    def spread(j):
+        over_x, over_core, from_x, _ = later_copies(j)
+        dy_arrived(oy, s, j)
+        over_x.start()
+        over_core.start()
+        dy_arrived(y, s_x, j)
+        from_x.start()
+        forward(1, j)
+    loop(0, planes, spread)
+    loop(planes, head, lambda n: forward(1, n))
+
+    def spread_far(j):
+        dy_arrived(oy, s_x, j)
+        later_copies(j)[3].start()
+        for hop in range(2, planes - 1):
+            forward(hop, j)
+        start_own(head + j)
+    loop(0, planes, spread_far)
+
+    def rest(n):
+        for hop in range(2, planes - 1):
+            forward(hop, n)
+        start_own(head + n)
+    loop(planes, head, rest)
+
+    def settle(j):
+        local_dy(j).wait()
+        for yy in (y, oy):
+            dy_arrived(yy, s_c, j)
+            dy_arrived(yy, s_xc, j)
+    loop(0, planes, settle)
+    dyup = pltpu.make_async_copy(dyv.at[:, s], dyup_ref, up_sem)
+    dyup.start()
+
+    block = min(512, tokens)
+
+    def product(yy, n, i):
+        start = pl.multiple_of(i * block, block)
+        total = None
+        for j in range(planes):
+            piece = lax.dot_general(
+                dyv[yy, j, pl.ds(start, block), :],
+                wv[j, pl.ds(pl.multiple_of(n * wide, wide), wide), :],
+                NT, preferred_element_type=jnp.float32)
+            total = piece if total is None else total + piece
+        return total, pl.ds(start, block)
+
+    def finish(n):
+        partial_copy(n).wait_recv()
+
+        def add(i):
+            at = pl.ds(pl.multiple_of(i * block, block), block)
+            acc[n % 2, at, :] = acc[n % 2, at, :] + prec[n, at, :].astype(jnp.float32)
+        loop(0, tokens // block, add)
+        out_copy(n).start()
+
+    def compute(n):
+        local_w(n).wait()
+
+        @pl.when(jnp.logical_not(inner))
+        def _():
+            for hop in range(1, planes):
+                @pl.when(z + hop < planes)
+                def _():
+                    w_arrived(z + hop, n)
+
+                @pl.when(z - hop >= 0)
+                def _():
+                    w_arrived(z - hop, n)
+
+        def other(i):
+            value, at = product(oy, n, i)
+            part[n, at, :] = value.astype(part.dtype)
+        loop(0, tokens // block, other)
+        partial_copy(n).start()
+
+        @pl.when(n >= 2)
+        def _():
+            out_copy(n - 2).wait()
+
+        def own(i):
+            value, at = product(y, n, i)
+            acc[n % 2, at, :] = value
+        loop(0, tokens // block, own)
+
+        @pl.when(n >= 1)
+        def _():
+            finish(n - 1)
+
+    def early(n):
+        forward(1, head + n)
+        compute(n)
+    loop(0, head, early)
+
+    def late(n):
+        for hop in range(2, planes - 1):
+            forward(hop, n)
+    loop(head, chunks, late)
+    loop(head, chunks, compute)
+    finish(chunks - 1)
+
+    out_copy(chunks - 2).wait()
+    out_copy(chunks - 1).wait()
+    dyup.wait()
+
+    def drain_dy(j):
+        for item in first_copies(j) + later_copies(j):
+            item.wait_send()
+    loop(0, planes, drain_dy)
+
+    def drain(n):
+        partial_copy(n).wait_send()
+
+        @pl.when(above)
+        def _():
+            w_send(z, n, True, True).wait_send()
+
+        @pl.when(below)
+        def _():
+            w_send(z, n, False, True).wait_send()
+
+        for hop in range(1, planes - 1):
+            @pl.when(jnp.logical_and(inner, z + hop < planes))
+            def _():
+                w_send(z + hop, n, False, False).wait_send()
+
+            @pl.when(jnp.logical_and(inner, z - hop >= 0))
+            def _():
+                w_send(z - hop, n, True, False).wait_send()
+    loop(0, chunks, drain)
+
+
+def dense_exchange(planes, gradient_rows, weight):
+    rows, width = gradient_rows.shape[0], weight.shape[1]
+    tokens, heads = rows * 4, weight.shape[0]
+    wide = min(256, heads // 8)
+    chunks = heads // wide
+    dma = pltpu.SemaphoreType.DMA
+    bf16, f32 = jnp.bfloat16, jnp.float32
+    return pl.pallas_call(
+        functools.partial(dense_kernel, planes, chunks, wide),
+        out_shape=(
+            jax.ShapeDtypeStruct((tokens, heads), f32),
+            jax.ShapeDtypeStruct((2, tokens, width), bf16),
+        ),
+        in_specs=[pl.BlockSpec(memory_space=pl.ANY)] * 2,
+        out_specs=[pl.BlockSpec(memory_space=pl.ANY)] * 2,
+        scratch_shapes=[
+            pltpu.VMEM((planes, heads, width), bf16),
+            pltpu.VMEM((2, planes, tokens, width), bf16),
+            pltpu.VMEM((chunks, tokens, wide), bf16),
+            pltpu.VMEM((chunks, tokens, wide), bf16),
+            pltpu.VMEM((2, tokens, wide), f32),
+            dma((chunks,)), dma((planes, chunks)), dma((planes, chunks)), dma((planes, chunks)),
+            dma((planes,)), dma((planes,)), dma((2, planes)), dma((4, planes)), dma((2, 4, planes)),
+            dma((chunks,)), dma((chunks,)), dma((2,)), dma,
+        ],
+        compiler_params=pltpu.CompilerParams(
+            collective_id=0, has_side_effects=True, vmem_limit_bytes=60 * 2**20),
+        cost_estimate=pl.CostEstimate(
+            flops=4 * tokens * heads * planes * width, bytes_accessed=2**27, transcendentals=0),
+    )(gradient_rows, weight)
+
+
+def line_body(
+    planes, stored_attention, output_gradient, output_weight, down_adapter, up_adapter, lengths, ranks
+):
+    attention_rows = stored_attention[0]
+    gradient_rows = output_gradient[0]
+    down_piece = down_adapter[0]
+    up_complete = up_adapter[0]
+    adapter_rank = ranks[0]
+    token_rows = attention_rows.shape[0]
+    y = lax.axis_index("trial") % 2
+    rank_mask = jnp.arange(up_complete.shape[0]) < adapter_rank
+    adapter_scale = adapter_alpha / jnp.sqrt(adapter_rank.astype(jnp.float32))
+    a_low = jnp.where(rank_mask[None, :], down_piece, jnp.zeros_like(down_piece))
+    b_low = jnp.where(rank_mask[:, None], up_complete, jnp.zeros_like(up_complete))
+    live = (jnp.arange(token_rows) < lengths[0])[:, None]
+    u_part = jnp.einsum(
+        "td,rd->tr", gradient_rows, b_low, preferred_element_type=jnp.float32
+    ).astype(jnp.bfloat16)
+    v_partial = jnp.dot(attention_rows, a_low, preferred_element_type=jnp.float32)
+    v_all = lax.psum(v_partial, "tensor").astype(jnp.bfloat16)
+    u_all = lax.all_gather(u_part, "tensor", axis=0, tiled=True)
+
+    dense, dy_cols = dense_exchange(planes, gradient_rows, output_weight)
+
+    u_all = jnp.where(live, u_all, jnp.zeros_like(u_all))
+    v_all = jnp.where(live, v_all, jnp.zeros_like(v_all))
+    pairs = [(2 * k + i, 2 * k + 1 - i) for k in range(planes) for i in range(2)]
+    v_other = lax.ppermute(v_all, "trial", pairs)
+    dy_mine = jnp.where(y == 0, dy_cols[0], dy_cols[1])
+    dy_other = jnp.where(y == 0, dy_cols[1], dy_cols[0])
+    up_given = jnp.einsum("tr,th->rh", v_other, dy_other, preferred_element_type=jnp.float32)
+    up_taken = lax.ppermute(up_given, "trial", pairs)
+    up_mine = jnp.einsum("tr,th->rh", v_all, dy_mine, preferred_element_type=jnp.float32)
+
+    lowrank_piece = jnp.einsum("tr,hr->th", u_all, a_low, preferred_element_type=jnp.float32)
+    attention_gradient = jnp.where(live, dense + adapter_scale * lowrank_piece, 0.0).astype(jnp.bfloat16)
+    down_total = jnp.einsum("th,tr->hr", attention_rows, u_all, preferred_element_type=jnp.float32)
+    up_total = jnp.concatenate(
+        [jnp.where(y == 0, up_mine, up_taken), jnp.where(y == 0, up_taken, up_mine)], axis=1)
+    down_gradient = adapter_scale * down_total / float(token_rows)
+    up_gradient = adapter_scale * up_total / float(token_rows)
+    return (attention_gradient[None], down_gradient[None], up_gradient[None])
 
 
 def body(
@@ -60,8 +411,13 @@
         P("trial"),
         P("trial"),
     )
+    trials, tensors = mesh.shape["trial"], mesh.shape["tensor"]
+    if tensors == 4 and trials == 2 * tensors:
+        run = functools.partial(line_body, trials // 2)
+    else:
+        run = body
     return jax.shard_map(
-        body,
+        run,
         mesh=mesh,
         in_specs=placed,
         out_specs=(

time: 826 us -> 353 us (0.43)
  waiting for transfers between devices: 707 us -> 7.82 us
  Pallas kernels: 0 us -> 292 us
  matrix products: 63.4 us -> 20.4 us
  between operations: 15.4 us -> 2.24 us
  blocking collectives: 34 us -> 24.4 us
    all_gather x2 -> x0, waiting for transfers between devices: 706 us -> none  [the longest x1 635 us: body(): lax.all_gather(output_weight, 'trial', axis=1, tiled=True)]
    pallas_call x0 -> x1, Pallas kernels: none -> 292 us  [dense_exchange(): pl.pallas_call(functools.partial(dense_kernel, planes, chunks, wide), out...]
    dot_general x6, matrix products: 63.4 us -> 20.4 us  [the longest x1 3.87 us: line_body(): jnp.dot(attention_rows, a_low, preferred_element_type=jnp.float32)]
  transfers between devices with their start and end apart: 2 -> 2, of which waited for: 2 -> 1; matrix products, arithmetic and copies ran while one was open for 2% -> 4% of each run, Pallas kernels for 0% -> 83%
where the time goes in v1:
time: 353 us; the launch traced here: 352 us
  Pallas kernels  292 us (83%)
  blocking collectives  24.4 us (7%)
  matrix products  20.4 us (6%)
  waiting for transfers between devices  7.82 us (2%)
    pallas_call x1, Pallas kernels, dense_exchange(): pl.pallas_call(functools.partial(dense_kernel, planes, chunks, wide), out...  292 us
    psum x1, blocking collectives, line_body(): v_all = lax.psum(v_partial, 'tensor').astype(jnp.bfloat16)  18.6 us
    ppermute x1, waiting for transfers between devices, line_body(): up_taken = lax.ppermute(up_given, 'trial', pairs)  7.82 us
  transfers between devices with their start and end apart: 2, of which 1 were waited for; matrix products, arithmetic and copies ran while one was open for 4% of the time, Pallas kernels for 83%

profile of v1, /device:TPU:0, one launch (start us, length us, event | category | flops | bytes accessed | tf_op | source)
XLA Modules:
  0.0 352.3 jit_solution(11731219940458169219)
XLA Ops:
  0.6 0.0 copy-start.2
  1.4 3.9 %fusion.30 = f32[1024,128]{0,1:T(8,128)S(1)} fusion(bf16[1,1024,2048]{2,1,0:T(8,128)(2,1)} %param.7, bf16[1,2048,128]{2,1,0:T(8,128)(2,1)} %param.10, pred[128]{0:T(512)(128)(4,1)S(1)} %iota_compare_fusion.1), kind=kOutput, calls=%fused_computation.25 | convolution fusion | flops 537133056 | bytes 5243008 | tf_op jit(solution)/shard_map/dot_general | solution.py:338
  5.3 18.6 %all-reduce.1 = bf16[1024,128]{0,1:T(8,128)(2,1)S(1)} all-reduce(f32[1024,128]{0,1:T(8,128)S(1)} %fusion.30), channel_id=1, replica_groups=mesh['trial'=8,'tensor'=4] {'tensor'}, use_global_device_ids=true, to_apply=%region_0.1 | all-reduce | flops 131072 | bytes 786432 | tf_op jit(solution)/shard_map/psum | solution.py:339
  24.6 1.6 collective-permute-start
  26.2 0.0 copy-done.2
  26.3 3.7 %fusion.36 = bf16[256,128]{0,1:T(8,128)(2,1)S(1)} fusion(bf16[1,128,8192]{2,1,0:T(8,128)(2,1)S(1)} %copy-done.2, pred[128]{0:T(512)(128)(4,1)S(1)} %iota_compare_fusion.1, bf16[1,256,8192]{2,1,0:T(8,128)(2,1)} %param.8), kind=kOutput, calls=%fused_computation.27 | convolution fusion | flops 537952256 | bytes 6357120 | tf_op jit(solution)/shard_map/td,rd->tr/dot_general | solution.py:335
  30.0 5.8 %all_gather.3 = bf16[1024,128]{0,1:T(8,128)(2,1)S(1)} all-gather(bf16[256,128]{0,1:T(8,128)(2,1)S(1)} %fusion.36), channel_id=1, replica_groups=mesh['trial'=8,'tensor'=4] {'tensor'}, dimensions={0}, use_global_device_ids=true | all-gather | bytes 327680 | tf_op jit(solution)/shard_map/all_gather | solution.py:340
  35.8 2.9 fusion.11
  38.7 1.3 copy.10
  40.0 291.7 %shard_map.94 = (f32[1024,2048]{1,0:T(8,128)}, bf16[2,1024,1024]{2,1,0:T(8,128)(2,1)}) custom-call(bf16[256,8192]{1,0:T(8,128)(2,1)} %bitcast.56, bf16[2048,1024]{1,0:T(8,128)(2,1)} %w_ref.1), custom_call_target="tpu_custom_call" | custom-call | flops 34359738368 | bytes 134217728 | tf_op jit(solution)/shard_map/pallas_call | solution.py:295
  331.8 0.0 copy-start
  331.8 3.0 fusion.16
  334.7 0.0 copy-start.1
  334.7 0.0 collective-permute-done
  334.8 3.5 fusion.14
  338.2 1.6 collective-permute-start.1
  339.8 0.0 copy-done
  339.8 0.0 copy-done.1
  339.8 3.5 fusion.4
  343.3 7.8 %collective-permute-done.1 = f32[128,1024]{1,0:T(8,128)S(1)} collective-permute-done((f32[128,1024]{1,0:T(8,128)S(1)}, f32[128,1024]{1,0:T(8,128)S(1)}, u32[]{:S(2)}, u32[]{:S(2)}) %collective-permute-start.1) | collective-permute-done | bytes 524320 | tf_op jit(solution)/shard_map/ppermute | solution.py:351
  351.1 0.1 select_bitcast_fusion.1
  351.2 1.1 fusion.39
  (3 shorter events, 0.0 us)
Async XLA Ops:
  0.6 25.6 %copy-start.2 = (bf16[1,128,8192]{2,1,0:T(8,128)(2,1)S(1)}, bf16[1,128,8192]{2,1,0:T(8,128)(2,1)}, u32[]{:S(2)}) copy-start(bf16[1,128,8192]{2,1,0:T(8,128)(2,1)} %param.11) | copy-start | bytes 6291460
  24.6 310.1 %collective-permute-start = (bf16[1024,128]{0,1:T(8,128)(2,1)S(1)}, bf16[1024,128]{0,1:T(8,128)(2,1)S(1)}, u32[]{:S(2)}, u32[]{:S(2)}) collective-permute-start(bf16[1024,128]{0,1:T(8,128)(2,1)S(1)} %convert_select_fusion), channel_id=1, source_target_pairs={{0,4},{4,0},{8,12},{12,8},{16,20},{20,16},{24,28},{28,24},{1,5},{5... | collective-permute-start | bytes 786440 | tf_op jit(solution)/shard_map/ppermute | solution.py:347
  331.8 8.0 %copy-start = (f32[1024,2048]{1,0:T(8,128)S(1)}, f32[1024,2048]{1,0:T(8,128)}, u32[]{:S(2)}) copy-start(f32[1024,2048]{1,0:T(8,128)} %get-tuple-element.5) | copy-start | bytes 25165828
  334.7 5.1 %copy-start.1 = (bf16[1,2048,128]{2,1,0:T(8,128)(2,1)S(1)}, bf16[1,2048,128]{2,1,0:T(8,128)(2,1)}, u32[]{:S(2)}) copy-start(bf16[1,2048,128]{2,1,0:T(8,128)(2,1)} %param.10) | copy-start | bytes 1572868
  338.2 12.8 %collective-permute-start.1 = (f32[128,1024]{1,0:T(8,128)S(1)}, f32[128,1024]{1,0:T(8,128)S(1)}, u32[]{:S(2)}, u32[]{:S(2)}) collective-permute-start(f32[128,1024]{1,0:T(8,128)S(1)} %fusion.14), channel_id=1, source_target_pairs={{0,4},{4,0},{8,12},{12,8},{16,20},{20,16},{24,28},{28,24},{1,5},{5... | collective-permute-start | bytes 1572872 | tf_op jit(solution)/shard_map/ppermute | solution.py:351

commit v2 on v1

--- a/solution.py
+++ b/solution.py
@@ -18,11 +18,12 @@
 
 def dense_kernel(
     planes, chunks, wide,
-    dy_ref, w_ref, dense_ref, dyup_ref,
-    wv, dyv, part, prec, acc,
+    dy_ref, w_ref, u_ref, v_ref, dense_ref, uall_ref, up_ref,
+    wv, dyv, part, prec, acc, uv, vparts, vsum, upv, upg,
     w_loc, w_up, w_dn, w_recv,
     dy_loc, dyy_send, dyx_send, dyc_send, dy_recv,
     p_send, p_recv, o_sem, up_sem,
+    low_loc, low_send, u_recv, v_recv, pair_send, pair_recv,
 ):
     trial, s = lax.axis_index("trial"), lax.axis_index("tensor")
     z, y = trial // 2, trial % 2
@@ -33,6 +34,7 @@
     tokens = dyv.shape[2]
     head = chunks // 2
     to_core, to_x, to_y = (trial, s_c), (trial, s_x), (2 * z + oy, s)
+    to_xc = (trial, s_xc)
     above, below = z < planes - 1, z > 0
     inner = jnp.logical_and(above, below)
 
@@ -118,6 +120,44 @@
         cols = pl.ds(pl.multiple_of(n * wide, wide), wide)
         return pltpu.make_async_copy(acc.at[n % 2], dense_ref.at[:, cols], o_sem.at[n % 2])
 
+    def u_slot(ss):
+        return uv.at[pl.ds(pl.multiple_of(ss * rows, rows), rows), :]
+
+    peers = ((to_core, s_c), (to_x, s_x), (to_xc, s_xc))
+
+    def low_copies():
+        return [
+            copy(src, dst, low_send.at[i, k], sem.at[s], dev)
+            for k, (dev, _) in enumerate(peers)
+            for i, (src, dst, sem) in enumerate(
+                ((u_ref, u_slot(s), u_recv), (v_ref, vparts.at[s], v_recv)))
+        ]
+
+    def low_local():
+        return (
+            pltpu.make_async_copy(u_ref, u_slot(s), low_loc.at[0]),
+            pltpu.make_async_copy(v_ref, vparts.at[s], low_loc.at[1]),
+        )
+
+    def low_settle():
+        for item in low_local():
+            item.wait()
+        for k, (dev, ss) in enumerate(peers):
+            copy(u_slot(ss), u_slot(ss), low_send.at[0, k], u_recv.at[ss], dev).wait_recv()
+            copy(vparts.at[ss], vparts.at[ss], low_send.at[1, k], v_recv.at[ss], dev).wait_recv()
+
+    def v_copy():
+        return copy(vsum.at[y], vsum.at[y], pair_send.at[0], pair_recv.at[0], to_y)
+
+    def up_copy():
+        return copy(upg, upv.at[y], pair_send.at[1], pair_recv.at[1], to_y)
+
+    def up_product(yy, put):
+        step = min(256, width)
+        for i in range(width // step):
+            at = pl.ds(i * step, step)
+            put(at, jnp.dot(vsum[yy], dyv[yy, s, :, at], preferred_element_type=jnp.float32))
+
     def loop(lo, hi, fn):
         def step(i, carry):
             fn(i)
@@ -125,7 +165,7 @@
         lax.fori_loop(lo, hi, step, 0)
 
     barrier = pltpu.get_barrier_semaphore()
-    for dev in (to_core, to_x, to_y):
+    for dev in (to_core, to_x, to_xc, to_y):
         pl.semaphore_signal(barrier, inc=1, device_id=dev, device_id_type=MESH)
 
     @pl.when(above)
@@ -138,11 +178,11 @@
 
     @pl.when(inner)
     def _():
-        pl.semaphore_wait(barrier, 5)
+        pl.semaphore_wait(barrier, 6)
 
     @pl.when(jnp.logical_not(inner))
     def _():
-        pl.semaphore_wait(barrier, 4)
+        pl.semaphore_wait(barrier, 5)
 
     loop(0, head, start_own)
 
@@ -152,6 +192,10 @@
         local_dy(j).start()
     loop(0, planes, begin)
     loop(0, chunks, lambda n: local_w(n).start())
+    for item in low_copies():
+        item.start()
+    for item in low_local():
+        item.start()
 
     def spread(j):
         over_x, over_core, from_x, _ = later_copies(j)
@@ -184,8 +228,19 @@
             dy_arrived(yy, s_c, j)
             dy_arrived(yy, s_xc, j)
     loop(0, planes, settle)
-    dyup = pltpu.make_async_copy(dyv.at[:, s], dyup_ref, up_sem)
-    dyup.start()
+    low_settle()
+    u_out = pltpu.make_async_copy(uv, uall_ref, up_sem.at[2])
+    u_out.start()
+    vsum[y] = (vparts[0] + vparts[1] + vparts[2] + vparts[3]).astype(vsum.dtype)
+    v_copy().start()
+
+    def put_own(at, value):
+        upv[y, :, at] = value
+    up_product(y, put_own)
+
+    def up_out(k):
+        return pltpu.make_async_copy(
+            upv.at[k], up_ref.at[:, pl.ds(pl.multiple_of(k * width, width), width)], up_sem.at[k])
 
     block = min(512, tokens)
 
@@ -250,13 +305,28 @@
     def late(n):
         for hop in range(2, planes - 1):
             forward(hop, n)
+    v_copy().wait_recv()
+
+    def put_given(at, value):
+        upg[:, at] = value
+    up_product(oy, put_given)
+    up_copy().start()
     loop(head, chunks, late)
+    up_copy().wait_recv()
+    up_out(y).start()
+    up_out(oy).start()
     loop(head, chunks, compute)
     finish(chunks - 1)
 
     out_copy(chunks - 2).wait()
     out_copy(chunks - 1).wait()
-    dyup.wait()
+    u_out.wait()
+    up_out(y).wait()
+    up_out(oy).wait()
+    for item in low_copies():
+        item.wait_send()
+    v_copy().wait_send()
+    up_copy().wait_send()
 
     def drain_dy(j):
         for item in first_copies(j) + later_copies(j):
@@ -285,9 +355,10 @@
     loop(0, chunks, drain)
 
 
-def dense_exchange(planes, gradient_rows, weight):
+def dense_exchange(planes, gradient_rows, weight, u_part, v_partial):
     rows, width = gradient_rows.shape[0], weight.shape[1]
     tokens, heads = rows * 4, weight.shape[0]
+    rank = u_part.shape[1]
     wide = min(256, heads // 8)
     chunks = heads // wide
     dma = pltpu.SemaphoreType.DMA
@@ -296,25 +367,32 @@
         functools.partial(dense_kernel, planes, chunks, wide),
         out_shape=(
             jax.ShapeDtypeStruct((tokens, heads), f32),
-            jax.ShapeDtypeStruct((2, tokens, width), bf16),
+            jax.ShapeDtypeStruct((tokens, rank), bf16),
+            jax.ShapeDtypeStruct((rank, 2 * width), f32),
         ),
-        in_specs=[pl.BlockSpec(memory_space=pl.ANY)] * 2,
-        out_specs=[pl.BlockSpec(memory_space=pl.ANY)] * 2,
+        in_specs=[pl.BlockSpec(memory_space=pl.ANY)] * 4,
+        out_specs=[pl.BlockSpec(memory_space=pl.ANY)] * 3,
         scratch_shapes=[
             pltpu.VMEM((planes, heads, width), bf16),
             pltpu.VMEM((2, planes, tokens, width), bf16),
             pltpu.VMEM((chunks, tokens, wide), bf16),
             pltpu.VMEM((chunks, tokens, wide), bf16),
             pltpu.VMEM((2, tokens, wide), f32),
+            pltpu.VMEM((tokens, rank), bf16),
+            pltpu.VMEM((4, rank, tokens), f32),
+            pltpu.VMEM((2, rank, tokens), bf16),
+            pltpu.VMEM((2, rank, width), f32),
+            pltpu.VMEM((rank, width), f32),
             dma((chunks,)), dma((planes, chunks)), dma((planes, chunks)), dma((planes, chunks)),
             dma((planes,)), dma((planes,)), dma((2, planes)), dma((4, planes)), dma((2, 4, planes)),
-            dma((chunks,)), dma((chunks,)), dma((2,)), dma,
+            dma((chunks,)), dma((chunks,)), dma((2,)), dma((3,)),
+            dma((2,)), dma((2, 3)), dma((4,)), dma((4,)), dma((2,)), dma((2,)),
         ],
         compiler_params=pltpu.CompilerParams(
             collective_id=0, has_side_effects=True, vmem_limit_bytes=60 * 2**20),
         cost_estimate=pl.CostEstimate(
             flops=4 * tokens * heads * planes * width, bytes_accessed=2**27, transcendentals=0),
-    )(gradient_rows, weight)
+    )(gradient_rows, weight, u_part, v_partial)
 
 
 def line_body(
@@ -326,36 +404,24 @@
     up_complete = up_adapter[0]
     adapter_rank = ranks[0]
     token_rows = attention_rows.shape[0]
-    y = lax.axis_index("trial") % 2
     rank_mask = jnp.arange(up_complete.shape[0]) < adapter_rank
     adapter_scale = adapter_alpha / jnp.sqrt(adapter_rank.astype(jnp.float32))
     a_low = jnp.where(rank_mask[None, :], down_piece, jnp.zeros_like(down_piece))
     b_low = jnp.where(rank_mask[:, None], up_complete, jnp.zeros_like(up_complete))
-    live = (jnp.arange(token_rows) < lengths[0])[:, None]
-    u_part = jnp.einsum(
-        "td,rd->tr", gradient_rows, b_low, preferred_element_type=jnp.float32
-    ).astype(jnp.bfloat16)
-    v_partial = jnp.dot(attention_rows, a_low, preferred_element_type=jnp.float32)
-    v_all = lax.psum(v_partial, "tensor").astype(jnp.bfloat16)
-    u_all = lax.all_gather(u_part, "tensor", axis=0, tiled=True)
-
-    dense, dy_cols = dense_exchange(planes, gradient_rows, output_weight)
-
-    u_all = jnp.where(live, u_all, jnp.zeros_like(u_all))
-    v_all = jnp.where(live, v_all, jnp.zeros_like(v_all))
-    pairs = [(2 * k + i, 2 * k + 1 - i) for k in range(planes) for i in range(2)]
-    v_other = lax.ppermute(v_all, "trial", pairs)
-    dy_mine = jnp.where(y == 0, dy_cols[0], dy_cols[1])
-    dy_other = jnp.where(y == 0, dy_cols[1], dy_cols[0])
-    up_given = jnp.einsum("tr,th->rh", v_other, dy_other, preferred_element_type=jnp.float32)
-    up_taken = lax.ppermute(up_given, "trial", pairs)
-    up_mine = jnp.einsum("tr,th->rh", v_all, dy_mine, preferred_element_type=jnp.float32)
+    live = jnp.arange(token_rows) < lengths[0]
+    shard_rows = gradient_rows.shape[0]
+    live_rows = lax.axis_index("tensor") * shard_rows + jnp.arange(shard_rows) < lengths[0]
+    u_part = jnp.einsum("td,rd->tr", gradient_rows, b_low, preferred_element_type=jnp.float32)
+    u_part = jnp.where(live_rows[:, None], u_part, 0.0).astype(jnp.bfloat16)
+    v_partial = jnp.einsum("tk,kr->rt", attention_rows, a_low, preferred_element_type=jnp.float32)
+    v_partial = jnp.where(live[None, :], v_partial, 0.0)
+
+    dense, u_all, up_total = dense_exchange(
+        planes, gradient_rows, output_weight, u_part, v_partial)
 
     lowrank_piece = jnp.einsum("tr,hr->th", u_all, a_low, preferred_element_type=jnp.float32)
-    attention_gradient = jnp.where(live, dense + adapter_scale * lowrank_piece, 0.0).astype(jnp.bfloat16)
+    attention_gradient = jnp.where(live[:, None], dense + adapter_scale * lowrank_piece, 0.0).astype(jnp.bfloat16)
     down_total = jnp.einsum("th,tr->hr", attention_rows, u_all, preferred_element_type=jnp.float32)
-    up_total = jnp.concatenate(
-        [jnp.where(y == 0, up_mine, up_taken), jnp.where(y == 0, up_taken, up_mine)], axis=1)
     down_gradient = adapter_scale * down_total / float(token_rows)
     up_gradient = adapter_scale * up_total / float(token_rows)
     return (attention_gradient[None], down_gradient[None], up_gradient[None])

time: 353 us -> 314 us (0.89)
  blocking collectives: 24.4 us -> 0 us
  waiting for transfers between devices: 7.82 us -> 0 us
  matrix products: 20.4 us -> 14.9 us
    psum x1 -> x0, blocking collectives: 18.6 us -> none  [line_body(): v_all = lax.psum(v_partial, 'tensor').astype(jnp.bfloat16)]
    dot_general x3 -> x1, matrix products: 10.3 us -> 2.32 us  [line_body(): jnp.einsum('tk,kr->rt', attention_rows, a_low, preferred_element_type=jnp...]
    ppermute x2 -> x0, waiting for transfers between devices: 7.82 us -> none  [the longest x1 7.82 us: line_body(): up_taken = lax.ppermute(up_given, 'trial', pairs)]
    all_gather x1 -> x0, blocking collectives: 5.79 us -> none  [line_body(): u_all = lax.all_gather(u_part, 'tensor', axis=0, tiled=True)]
  transfers between devices with their start and end apart: 2 -> 0, of which waited for: 1 -> 0; matrix products, arithmetic and copies ran while one was open for 4% -> 0% of each run, Pallas kernels for 83% -> 0%
where the time goes in v2:
time: 314 us
  Pallas kernels  294 us (94%)
  matrix products  14.9 us (5%)
    pallas_call x1, Pallas kernels, dense_exchange(): pl.pallas_call(functools.partial(dense_kernel, planes, chunks, wide), out...  294 us
    dot_general x1, matrix products, line_body(): jnp.einsum('tr,hr->th', u_all, a_low, preferred_element_type=jnp.float32)  6.9 us

profile of v2, /device:TPU:0, one launch (start us, length us, event | category | flops | bytes accessed | tf_op | source)
XLA Modules:
  0.0 314.0 jit_solution(11227340167542864838)
XLA Ops:
  0.6 0.0 copy-start.2
  1.4 0.0 copy-start
  2.2 5.0 %fusion.27.u_ref = bf16[256,128]{1,0:T(8,128)(2,1)} fusion(bf16[1,128,8192]{2,1,0:T(8,128)(2,1)} %param.11, pred[128]{0:T(512)(128)(4,1)S(1)} %iota_compare_fusion.1, pred[256]{0:T(512)(128)(4,1)S(1)} %add_compare_fusion, bf16[1,256,8192]{2,1,0:T(8,128)(2,1)} %param.8), kind=kOutput, calls=%fused_computation.16 | convolution fusion | flops 537985024 | bytes 6357376 | tf_op jit(solution)/shard_map/td,rd->tr/dot_general | solution.py:414
  7.2 0.0 copy-done.2
  7.2 0.0 copy-done
  7.2 2.3 fusion.18.v_ref
  9.5 294.4 %shard_map.94 = (f32[1024,2048]{1,0:T(8,128)}, bf16[1024,128]{1,0:T(8,128)(2,1)}, f32[128,2048]{1,0:T(8,128)}) custom-call(bf16[256,8192]{1,0:T(8,128)(2,1)} %bitcast.49, bf16[2048,1024]{1,0:T(8,128)(2,1)} %w_ref.1, bf16[256,128]{1,0:T(8,128)(2,1)} %fusion.27.u_ref, f32[128,1024]{1,0:T(8,128)} %fusion.18.v_ref), custom_call_target="tpu_custom_call" | custom-call | flops 34359738368 | bytes 134217728 | tf_op jit(solution)/shard_map/pallas_call | solution.py:366
  303.9 0.0 copy-start.4
  303.9 0.0 copy-start.1
  303.9 0.0 copy-start.3
  303.9 6.9 %fusion.4 = bf16[1,1024,2048]{2,1,0:T(8,128)(2,1)} fusion(f32[1024,2048]{1,0:T(8,128)} %get-tuple-element.6, bf16[1024,128]{1,0:T(8,128)(2,1)} %get-tuple-element.7, f32[]{:T(128)S(6)} %div.15, pred[1024]{0:T(1024)(128)(4,1)S(1)} %iota_compare_fusion, bf16[1,2048,128]{2,1,0:T(8,128)(2,1)S(1)} %copy-done.2, pred[128]{0:T(512)(128)(4,1)S(1)} %iota_compare_fusion.1), kind=kOutput, calls=%fused_computation.5 | convolution fusion | flops 545521664 | bytes 13370500 | tf_op jit(solution)/shard_map/tr,hr->th/dot_general | solution.py:422
  310.9 0.0 copy-done.4
  310.9 1.1 multiply_bitcast_fusion
  311.9 0.0 copy-done.1
  311.9 0.0 copy-done.3
  311.9 0.7 fusion.11
  312.7 1.3 copy.11
  (3 shorter events, 0.0 us)
Async XLA Ops:
  0.6 6.6 %copy-start.2 = (bf16[1,2048,128]{2,1,0:T(8,128)(2,1)S(1)}, bf16[1,2048,128]{2,1,0:T(8,128)(2,1)}, u32[]{:S(2)}) copy-start(bf16[1,2048,128]{2,1,0:T(8,128)(2,1)} %param.10) | copy-start | bytes 1572868
  1.4 5.8 %copy-start = (bf16[1,1024,2048]{2,1,0:T(8,128)(2,1)S(1)}, bf16[1,1024,2048]{2,1,0:T(8,128)(2,1)}, u32[]{:S(2)}) copy-start(bf16[1,1024,2048]{2,1,0:T(8,128)(2,1)} %param.7) | copy-start | bytes 12582916
  303.9 6.9 %copy-start.4 = (f32[128,2048]{1,0:T(8,128)S(1)}, f32[128,2048]{1,0:T(8,128)}, u32[]{:S(2)}) copy-start(f32[128,2048]{1,0:T(8,128)} %get-tuple-element.8) | copy-start | bytes 3145732
  303.9 8.0 %copy-start.1 = (bf16[1,1024,2048]{2,1,0:T(8,128)(2,1)S(1)}, bf16[1,1024,2048]{2,1,0:T(8,128)(2,1)}, u32[]{:S(2)}) copy-start(bf16[1,1024,2048]{2,1,0:T(8,128)(2,1)} %param.7) | copy-start | bytes 12582916
  303.9 8.0 %copy-start.3 = (bf16[1024,128]{1,0:T(8,128)(2,1)S(1)}, bf16[1024,128]{1,0:T(8,128)(2,1)}, u32[]{:S(2)}) copy-start(bf16[1024,128]{1,0:T(8,128)(2,1)} %get-tuple-element.7) | copy-start | bytes 786436

commit v3 on v2

--- a/solution.py
+++ b/solution.py
@@ -18,12 +18,12 @@
 
 def dense_kernel(
     planes, chunks, wide,
-    dy_ref, w_ref, u_ref, v_ref, dense_ref, uall_ref, up_ref,
-    wv, dyv, part, prec, acc, uv, vparts, vsum, upv, upg,
+    dy_ref, w_ref, att_ref, a_ref, b_ref, mask_ref, dense_ref, uall_ref, up_ref,
+    wv, dyv, part, prec, acc, uv, vparts, vsum, upv, upg, dyo, attv, av, bv,
     w_loc, w_up, w_dn, w_recv,
     dy_loc, dyy_send, dyx_send, dyc_send, dy_recv,
     p_send, p_recv, o_sem, up_sem,
-    low_loc, low_send, u_recv, v_recv, pair_send, pair_recv,
+    far_loc, low_loc, low_send, u_recv, v_recv, pair_send, pair_recv,
 ):
     trial, s = lax.axis_index("trial"), lax.axis_index("tensor")
     z, y = trial // 2, trial % 2
@@ -113,8 +113,11 @@
             dy_send(dy_slot(oy, s_x, j), oy, s_x, j, dyc_send.at[3, j], to_core),
         )
 
-    def partial_copy(n):
-        return copy(part.at[n], prec.at[n], p_send.at[n], p_recv.at[n], to_y)
+    block = min(512, tokens)
+
+    def partial_copy(n, i):
+        at = pl.ds(pl.multiple_of(i * block, block), block)
+        return copy(part.at[n, at, :], prec.at[n, at, :], p_send.at[n, i], p_recv.at[n, i], to_y)
 
     def out_copy(n):
         cols = pl.ds(pl.multiple_of(n * wide, wide), wide)
@@ -130,18 +133,41 @@
             copy(src, dst, low_send.at[i, k], sem.at[s], dev)
             for k, (dev, _) in enumerate(peers)
             for i, (src, dst, sem) in enumerate(
-                ((u_ref, u_slot(s), u_recv), (v_ref, vparts.at[s], v_recv)))
+                ((u_slot(s), u_slot(s), u_recv), (vparts.at[s], vparts.at[s], v_recv)))
         ]
 
     def low_local():
         return (
-            pltpu.make_async_copy(u_ref, u_slot(s), low_loc.at[0]),
-            pltpu.make_async_copy(v_ref, vparts.at[s], low_loc.at[1]),
+            pltpu.make_async_copy(b_ref, bv, low_loc.at[0]),
+            pltpu.make_async_copy(att_ref, attv, low_loc.at[1]),
+            pltpu.make_async_copy(a_ref, av, low_loc.at[2]),
         )
 
-    def low_settle():
+    def far_dy(j):
+        return pltpu.make_async_copy(dy_own(j, oy), dyo.at[j], far_loc.at[j])
+
+    def low_compute():
         for item in low_local():
             item.wait()
+        step = min(256, tokens)
+
+        def v_rows(i):
+            at = pl.ds(pl.multiple_of(i * step, step), step)
+            value = jnp.dot(attv[at, :], av[...], preferred_element_type=jnp.float32)
+            vparts[s, :, at] = value.T * mask_ref[:, at]
+        loop(0, tokens // step, v_rows)
+        total = None
+        for j in range(planes):
+            local_dy(j).wait()
+            far_dy(j).wait()
+            mine = dyv[y, j, pl.ds(pl.multiple_of(s * rows, rows), rows), :]
+            for value, parity in ((mine, y), (dyo[j], oy)):
+                at = pl.ds(pl.multiple_of((2 * j + parity) * width, width), width)
+                piece = lax.dot_general(value, bv[:, at], NT, preferred_element_type=jnp.float32)
+                total = piece if total is None else total + piece
+        uv[pl.ds(pl.multiple_of(s * rows, rows), rows), :] = total.astype(uv.dtype)
+
+    def low_settle():
         for k, (dev, ss) in enumerate(peers):
             copy(u_slot(ss), u_slot(ss), low_send.at[0, k], u_recv.at[ss], dev).wait_recv()
             copy(vparts.at[ss], vparts.at[ss], low_send.at[1, k], v_recv.at[ss], dev).wait_recv()
@@ -192,9 +218,11 @@
         local_dy(j).start()
     loop(0, planes, begin)
     loop(0, chunks, lambda n: local_w(n).start())
+    for item in low_local():
+        item.start()
+    loop(0, planes, lambda j: far_dy(j).start())
+    low_compute()
     for item in low_copies():
-        item.start()
-    for item in low_local():
         item.start()
 
     def spread(j):
@@ -223,7 +251,6 @@
     loop(planes, head, rest)
 
     def settle(j):
-        local_dy(j).wait()
         for yy in (y, oy):
             dy_arrived(yy, s_c, j)
             dy_arrived(yy, s_xc, j)
@@ -241,8 +268,6 @@
     def up_out(k):
         return pltpu.make_async_copy(
             upv.at[k], up_ref.at[:, pl.ds(pl.multiple_of(k * width, width), width)], up_sem.at[k])
-
-    block = min(512, tokens)
 
     def product(yy, n, i):
         start = pl.multiple_of(i * block, block)
@@ -256,9 +281,8 @@
         return total, pl.ds(start, block)
 
     def finish(n):
-        partial_copy(n).wait_recv()
-
         def add(i):
+            partial_copy(n, i).wait_recv()
             at = pl.ds(pl.multiple_of(i * block, block), block)
             acc[n % 2, at, :] = acc[n % 2, at, :] + prec[n, at, :].astype(jnp.float32)
         loop(0, tokens // block, add)
@@ -281,8 +305,8 @@
         def other(i):
             value, at = product(oy, n, i)
             part[n, at, :] = value.astype(part.dtype)
+            partial_copy(n, i).start()
         loop(0, tokens // block, other)
-        partial_copy(n).start()
 
         @pl.when(n >= 2)
         def _():
@@ -334,7 +358,7 @@
     loop(0, planes, drain_dy)
 
     def drain(n):
-        partial_copy(n).wait_send()
+        loop(0, tokens // block, lambda i: partial_copy(n, i).wait_send())
 
         @pl.when(above)
         def _():
@@ -355,10 +379,12 @@
     loop(0, chunks, drain)
 
 
-def dense_exchange(planes, gradient_rows, weight, u_part, v_partial):
+def dense_exchange(planes, gradient_rows, weight, attention, down, up, live):
     rows, width = gradient_rows.shape[0], weight.shape[1]
     tokens, heads = rows * 4, weight.shape[0]
-    rank = u_part.shape[1]
+    rank = up.shape[0]
+    halves = max(1, tokens // 512)
+    any_space, vmem = pl.BlockSpec(memory_space=pl.ANY), pl.BlockSpec(memory_space=pltpu.VMEM)
     wide = min(256, heads // 8)
     chunks = heads // wide
     dma = pltpu.SemaphoreType.DMA
@@ -370,8 +396,8 @@
             jax.ShapeDtypeStruct((tokens, rank), bf16),
             jax.ShapeDtypeStruct((rank, 2 * width), f32),
         ),
-        in_specs=[pl.BlockSpec(memory_space=pl.ANY)] * 4,
-        out_specs=[pl.BlockSpec(memory_space=pl.ANY)] * 3,
+        in_specs=[any_space] * 5 + [vmem],
+        out_specs=[any_space] * 3,
         scratch_shapes=[
             pltpu.VMEM((planes, heads, width), bf16),
             pltpu.VMEM((2, planes, tokens, width), bf16),
@@ -383,16 +409,20 @@
             pltpu.VMEM((2, rank, tokens), bf16),
             pltpu.VMEM((2, rank, width), f32),
             pltpu.VMEM((rank, width), f32),
+            pltpu.VMEM((planes, rows, width), bf16),
+            pltpu.VMEM(attention.shape, bf16),
+            pltpu.VMEM(down.shape, bf16),
+            pltpu.VMEM(up.shape, bf16),
             dma((chunks,)), dma((planes, chunks)), dma((planes, chunks)), dma((planes, chunks)),
             dma((planes,)), dma((planes,)), dma((2, planes)), dma((4, planes)), dma((2, 4, planes)),
-            dma((chunks,)), dma((chunks,)), dma((2,)), dma((3,)),
-            dma((2,)), dma((2, 3)), dma((4,)), dma((4,)), dma((2,)), dma((2,)),
+            dma((chunks, halves)), dma((chunks, halves)), dma((2,)), dma((3,)),
+            dma((planes,)), dma((3,)), dma((2, 3)), dma((4,)), dma((4,)), dma((2,)), dma((2,)),
         ],
         compiler_params=pltpu.CompilerParams(
             collective_id=0, has_side_effects=True, vmem_limit_bytes=60 * 2**20),
         cost_estimate=pl.CostEstimate(
             flops=4 * tokens * heads * planes * width, bytes_accessed=2**27, transcendentals=0),
-    )(gradient_rows, weight, u_part, v_partial)
+    )(gradient_rows, weight, attention, down, up, live)
 
 
 def line_body(
@@ -407,17 +437,12 @@
     rank_mask = jnp.arange(up_complete.shape[0]) < adapter_rank
     adapter_scale = adapter_alpha / jnp.sqrt(adapter_rank.astype(jnp.float32))
     a_low = jnp.where(rank_mask[None, :], down_piece, jnp.zeros_like(down_piece))
-    b_low = jnp.where(rank_mask[:, None], up_complete, jnp.zeros_like(up_complete))
     live = jnp.arange(token_rows) < lengths[0]
-    shard_rows = gradient_rows.shape[0]
-    live_rows = lax.axis_index("tensor") * shard_rows + jnp.arange(shard_rows) < lengths[0]
-    u_part = jnp.einsum("td,rd->tr", gradient_rows, b_low, preferred_element_type=jnp.float32)
-    u_part = jnp.where(live_rows[:, None], u_part, 0.0).astype(jnp.bfloat16)
-    v_partial = jnp.einsum("tk,kr->rt", attention_rows, a_low, preferred_element_type=jnp.float32)
-    v_partial = jnp.where(live[None, :], v_partial, 0.0)
-
     dense, u_all, up_total = dense_exchange(
-        planes, gradient_rows, output_weight, u_part, v_partial)
+        planes, gradient_rows, output_weight, attention_rows, down_piece, up_complete,
+        live.astype(jnp.float32)[None, :])
+    u_all = jnp.where(live[:, None] & rank_mask[None, :], u_all, jnp.zeros_like(u_all))
+    up_total = jnp.where(rank_mask[:, None], up_total, 0.0)
 
     lowrank_piece = jnp.einsum("tr,hr->th", u_all, a_low, preferred_element_type=jnp.float32)
     attention_gradient = jnp.where(live[:, None], dense + adapter_scale * lowrank_piece, 0.0).astype(jnp.bfloat16)

time: 314 us -> 307 us (0.978)
  matrix products: 14.9 us -> 7.8 us
    dot_general x2 -> x0, matrix products: 7.28 us -> none  [the longest x1 4.97 us: line_body(): jnp.einsum('td,rd->tr', gradient_rows, b_low, preferred_element_type=jnp....]
where the time goes in v3:
time: 307 us
  Pallas kernels  294 us (96%)
  matrix products  7.8 us (3%)
    pallas_call x1, Pallas kernels, dense_exchange(): pl.pallas_call(functools.partial(dense_kernel, planes, chunks, wide), out...  294 us
    dot_general x1, matrix products, line_body(): jnp.einsum('tr,hr->th', u_all, a_low, preferred_element_type=jnp.float32)  6.97 us

profile of v3, /device:TPU:0, one launch (start us, length us, event | category | flops | bytes accessed | tf_op | source)
XLA Modules:
  0.0 307.0 jit_solution(11292590923955132537)
XLA Ops:
  2.0 0.6 compare_convert_fusion.mask_ref
  2.6 0.0 copy-start.3
  2.6 294.1 %shard_map.94 = (f32[1024,2048]{1,0:T(8,128)}, bf16[1024,128]{1,0:T(8,128)(2,1)}, f32[128,2048]{1,0:T(8,128)}) custom-call(bf16[256,8192]{1,0:T(8,128)(2,1)} %bitcast.26, bf16[2048,1024]{1,0:T(8,128)(2,1)} %w_ref.1, bf16[1024,2048]{1,0:T(8,128)(2,1)} %bitcast.24, bf16[2048,128]{1,0:T(8,128)(2,1)} %bitcast.25, bf16[128,8192]{1,0:T(8,128)(2,1)} %bitcast.27, ...), custom_call_target="tpu_custom_call" | custom-call | flops 34359738368 | bytes 134217728 | tf_op jit(solution)/shard_map/pallas_call | solution.py:392
  296.7 0.0 copy-done.3
  296.7 0.0 copy-start.2
  296.7 0.0 copy-start
  296.7 0.0 copy-start.1
  296.7 7.0 %fusion = bf16[1,1024,2048]{2,1,0:T(8,128)(2,1)} fusion(f32[1024,2048]{1,0:T(8,128)} %get-tuple-element.6, f32[]{:T(128)S(6)} %div.15, pred[1024]{0:T(1024)(128)(4,1)S(1)} %iota_compare_fusion, pred[128]{0:T(512)(128)(4,1)S(1)} %iota_compare_fusion.1, bf16[1024,128]{1,0:T(8,128)(2,1)} %get-tuple-element.7, bf16[1,2048,128]{2,1,0:T(8,128)(2,1)S(1)} %copy-done.3), kind=kOutput, calls=%fused_computation.1 | convolution fusion | flops 545783808 | bytes 13370500 | tf_op jit(solution)/shard_map/tr,hr->th/dot_general | solution.py:447
  303.7 0.0 copy-done.2
  303.7 1.1 multiply_bitcast_fusion
  304.8 0.0 copy-done
  304.8 0.0 copy-done.1
  304.8 0.8 fusion.2
  305.7 1.3 copy.10
  (2 shorter events, 0.0 us)
Async XLA Ops:
  2.6 294.1 %copy-start.3 = (bf16[1,2048,128]{2,1,0:T(8,128)(2,1)S(1)}, bf16[1,2048,128]{2,1,0:T(8,128)(2,1)}, u32[]{:S(2)}) copy-start(bf16[1,2048,128]{2,1,0:T(8,128)(2,1)} %param.10) | copy-start | bytes 1572868
  296.7 7.0 %copy-start.2 = (f32[128,2048]{1,0:T(8,128)S(1)}, f32[128,2048]{1,0:T(8,128)}, u32[]{:S(2)}) copy-start(f32[128,2048]{1,0:T(8,128)} %get-tuple-element.8) | copy-start | bytes 3145732
  296.7 8.1 %copy-start = (bf16[1,1024,2048]{2,1,0:T(8,128)(2,1)S(1)}, bf16[1,1024,2048]{2,1,0:T(8,128)(2,1)}, u32[]{:S(2)}) copy-start(bf16[1,1024,2048]{2,1,0:T(8,128)(2,1)} %param.7) | copy-start | bytes 12582916
  296.7 8.1 %copy-start.1 = (bf16[1024,128]{1,0:T(8,128)(2,1)S(1)}, bf16[1024,128]{1,0:T(8,128)(2,1)}, u32[]{:S(2)}) copy-start(bf16[1024,128]{1,0:T(8,128)(2,1)} %get-tuple-element.7) | copy-start | bytes 786436

commit v4 on v3

--- a/solution.py
+++ b/solution.py
@@ -385,7 +385,7 @@
     rank = up.shape[0]
     halves = max(1, tokens // 512)
     any_space, vmem = pl.BlockSpec(memory_space=pl.ANY), pl.BlockSpec(memory_space=pltpu.VMEM)
-    wide = min(256, heads // 8)
+    wide = min(128, heads // 8)
     chunks = heads // wide
     dma = pltpu.SemaphoreType.DMA
     bf16, f32 = jnp.bfloat16, jnp.float32

time: 307 us -> 303 us (0.987)
  Pallas kernels: 294 us -> 290 us
    pallas_call x1, Pallas kernels: 294 us -> 290 us  [dense_exchange(): pl.pallas_call(functools.partial(dense_kernel, planes, chunks, wide), out...]
where the time goes in v4:
time: 303 us
  Pallas kernels  290 us (96%)
  matrix products  7.8 us (3%)
    pallas_call x1, Pallas kernels, dense_exchange(): pl.pallas_call(functools.partial(dense_kernel, planes, chunks, wide), out...  290 us
    dot_general x1, matrix products, line_body(): jnp.einsum('tr,hr->th', u_all, a_low, preferred_element_type=jnp.float32)  6.97 us

profile of v4, /device:TPU:0, one launch (start us, length us, event | category | flops | bytes accessed | tf_op | source)
XLA Modules:
  0.0 302.6 jit_solution(15141227044735099770)
XLA Ops:
  2.0 0.6 compare_convert_fusion.mask_ref
  2.6 0.0 copy-start.3
  2.6 289.7 %shard_map.94 = (f32[1024,2048]{1,0:T(8,128)}, bf16[1024,128]{1,0:T(8,128)(2,1)}, f32[128,2048]{1,0:T(8,128)}) custom-call(bf16[256,8192]{1,0:T(8,128)(2,1)} %bitcast.26, bf16[2048,1024]{1,0:T(8,128)(2,1)} %w_ref.1, bf16[1024,2048]{1,0:T(8,128)(2,1)} %bitcast.24, bf16[2048,128]{1,0:T(8,128)(2,1)} %bitcast.25, bf16[128,8192]{1,0:T(8,128)(2,1)} %bitcast.27, ...), custom_call_target="tpu_custom_call" | custom-call | flops 34359738368 | bytes 134217728 | tf_op jit(solution)/shard_map/pallas_call | solution.py:392
  292.3 0.0 copy-done.3
  292.3 0.0 copy-start.2
  292.3 0.0 copy-start
  292.3 0.0 copy-start.1
  292.3 7.0 %fusion = bf16[1,1024,2048]{2,1,0:T(8,128)(2,1)} fusion(f32[1024,2048]{1,0:T(8,128)} %get-tuple-element.6, f32[]{:T(128)S(6)} %div.15, pred[1024]{0:T(1024)(128)(4,1)S(1)} %iota_compare_fusion, pred[128]{0:T(512)(128)(4,1)S(1)} %iota_compare_fusion.1, bf16[1024,128]{1,0:T(8,128)(2,1)} %get-tuple-element.7, bf16[1,2048,128]{2,1,0:T(8,128)(2,1)S(1)} %copy-done.3), kind=kOutput, calls=%fused_computation.1 | convolution fusion | flops 545783808 | bytes 13370500 | tf_op jit(solution)/shard_map/tr,hr->th/dot_general | solution.py:447
  299.3 0.0 copy-done.2
  299.3 1.1 multiply_bitcast_fusion
  300.4 0.0 copy-done
  300.4 0.0 copy-done.1
  300.4 0.8 fusion.2
  301.3 1.3 copy.10
  (2 shorter events, 0.0 us)
Async XLA Ops:
  2.6 289.7 %copy-start.3 = (bf16[1,2048,128]{2,1,0:T(8,128)(2,1)S(1)}, bf16[1,2048,128]{2,1,0:T(8,128)(2,1)}, u32[]{:S(2)}) copy-start(bf16[1,2048,128]{2,1,0:T(8,128)(2,1)} %param.10) | copy-start | bytes 1572868
  292.3 7.0 %copy-start.2 = (f32[128,2048]{1,0:T(8,128)S(1)}, f32[128,2048]{1,0:T(8,128)}, u32[]{:S(2)}) copy-start(f32[128,2048]{1,0:T(8,128)} %get-tuple-element.8) | copy-start | bytes 3145732
  292.3 8.1 %copy-start = (bf16[1,1024,2048]{2,1,0:T(8,128)(2,1)S(1)}, bf16[1,1024,2048]{2,1,0:T(8,128)(2,1)}, u32[]{:S(2)}) copy-start(bf16[1,1024,2048]{2,1,0:T(8,128)(2,1)} %param.7) | copy-start | bytes 12582916
  292.3 8.1 %copy-start.1 = (bf16[1024,128]{1,0:T(8,128)(2,1)S(1)}, bf16[1024,128]{1,0:T(8,128)(2,1)}, u32[]{:S(2)}) copy-start(bf16[1024,128]{1,0:T(8,128)(2,1)} %get-tuple-element.7) | copy-start | bytes 786436
